TPU v7x, 1024 devices: a whole 4x4x32 slice. The times are simulated.
1024 devices in a mesh: inpair: 32 (over y, z_hi, core), outpair: 32 (over z_lo, x).
Axes of the slice: x: 4, y: 4, z: 32 (z_hi: 4, z_lo: 8; z = z_hi * 8 + z_lo), core: 2. Of those that a mesh axis runs over, the one named last changes fastest.
Arguments:
- integrals: bfloat16 [32768, 32768], P('inpair', 'outpair'), may hold values from -0.03125 to 0.03125
- amplitudes: bfloat16 [32, 512, 32768], P('outpair', None, 'inpair'), may hold values from -6 to 6
- tile_live: int32 [128, 128], P('inpair', 'outpair'), may hold values 0 or 1
- batch_owner: int32 [2], replicated, may hold values from 0 to 31
- occ_energy: float32 [2, 512], P(None, 'inpair'), may hold values from -2 to -0.5
- vir_energy: float32 [32768], P('outpair'), may hold values from 0.5 to 4
- swap_within: int32 [32], replicated, may hold values from 0 to 31, each once
Outputs:
- update: float32 [2, 512, 32768], P(None, 'inpair', 'outpair')
Inputs may be any that keep to these rules, and one draw needn't show every extreme that they name: `swap_within`: each value once.
All inputs are finite; a program needn't handle non-finite values. No bound on the sum of `tile_live` on one device may be relied on, other than what follows from the above.
Results may differ from a plain program's by a relative error of at most 0.0003.
Values may be sent and summed in bfloat16 or wider, within the bound.
A program may use at most 32 MiB of HBM per device.

v0:
```python
import jax
import jax.numpy as jnp
from jax import lax
from jax.sharding import PartitionSpec as P

SUB_R = 256
SUB_C = 256
NB = 2


def spread(block, axis, holder):
    block = jnp.where(lax.axis_index(axis) == holder, block, jnp.zeros_like(block))
    return lax.psum(block, axis)


def on_device(integrals, amplitudes, tile_live, batch_owner, occ_energy, vir_energy, swap_within):
    parties = lax.axis_size("outpair")
    tile_mask = jnp.repeat(jnp.repeat(tile_live, SUB_R, 0), SUB_C, 1).astype(jnp.bfloat16)
    weights = integrals * tile_mask
    batches = []
    for index in range(NB):
        batches.append(spread(amplitudes[0], "outpair", batch_owner[index]))
    results = []
    for index in range(NB):
        partial_value = jnp.dot(batches[index], weights, preferred_element_type=jnp.float32)
        results.append(lax.psum_scatter(partial_value, "inpair", scatter_dimension=0, tiled=True))
    summed = jnp.stack(results)
    local_rows = summed.shape[1]
    width = summed.shape[2]
    pair_grid = summed.reshape(NB, local_rows, parties, width // parties)
    received = lax.all_to_all(pair_grid, "outpair", split_axis=2, concat_axis=2, tiled=True)
    swapped = jnp.take(received, swap_within, axis=3).reshape(NB, local_rows, width)
    denominator = vir_energy[None, None, :] - occ_energy[:, :, None]
    return (summed + swapped) / denominator


def solution(mesh):
    return jax.shard_map(
        on_device,
        mesh=mesh,
        in_specs=(
            P("inpair", "outpair"),
            P("outpair", None, "inpair"),
            P("inpair", "outpair"),
            P(),
            P(None, "inpair"),
            P("outpair"),
            P(),
        ),
        out_specs=P(None, "inpair", "outpair"),
        check_vma=False,
    )
```

profile of v0, /device:TPU:8, one launch (start us, length us, event | category | flops | bytes accessed | tf_op | source)
XLA Modules:
  0.0 906.4 jit_solution(8694106809761405423)
XLA Ops:
  6.5 0.0 all-reduce.3.cloned.1.call-start
  6.5 1.3 fusion.5
  9.2 0.0 copy-start.4
  9.2 2.7 select_bitcast_fusion.1
  11.9 0.0 all-reduce.3.cloned.1.call-update
  11.9 0.0 reduce-scatter.3.cloned.1.call-start
  11.9 0.0 copy-done.4
  12.0 1.2 broadcast_in_dim.25
  13.3 0.5 copy.19
  13.8 487.0 %all-reduce.3.cloned.1.call-done = (bf16[512,1024]{1,0:T(8,128)(2,1)}, bf16[512,1024]{1,0:T(8,128)(2,1)}) async-done(((bf16[512,1024]{1,0:T(8,128)(2,1)}, bf16[512,1024]{1,0:T(8,128)(2,1)}), (bf16[512,1024]{1,0:T(8,128)(2,1)}, bf16[512,1024]{1,0:T(8,128)(2,1)})) %all-reduce.3.cloned.1.call-update) | async-done | bytes 2097168 | tf_op jit(solution)/shard_map/psum | solution.py:13
  500.8 4.5 fusion.2
  505.3 0.0 copy-start
  505.3 0.0 reduce-scatter.3.cloned.1.call-update
  505.3 0.0 reduce-scatter.5.cloned.1.call-start
  505.3 1.1 copy-done
  506.5 4.2 fusion
  510.7 0.0 reduce-scatter.5.cloned.1.call-update
  510.7 0.0 copy-start.6
  510.7 178.9 %reduce-scatter.3.cloned.1.call-done = f32[16,1024]{1,0:T(8,128)} async-done(((f32[512,1024]{1,0:T(8,128)}), f32[16,1024]{1,0:T(8,128)}) %reduce-scatter.3.cloned.1.call-update) | async-done | bytes 65552 | tf_op jit(solution)/shard_map/reduce_scatter | solution.py:26
  689.6 1.0 stack.18
  690.6 0.2 copy.15
  690.7 178.9 %reduce-scatter.5.cloned.1.call-done = f32[16,1024]{1,0:T(8,128)} async-done(((f32[512,1024]{1,0:T(8,128)}), f32[16,1024]{1,0:T(8,128)}) %reduce-scatter.5.cloned.1.call-update) | async-done | bytes 65552 | tf_op jit(solution)/shard_map/reduce_scatter | solution.py:26
  869.7 1.0 stack.19
  870.6 0.2 copy.16
  870.8 0.9 reshape.34
  871.8 10.8 %all-to-all-start = ((f32[32,1,1024]{2,1,0:T(1,128)}), f32[32,1,1024]{2,1,0:T(1,128)S(1)}, u32[]{:S(2)}, u32[]{:S(2)}) async-start(f32[32,1,1024]{2,1,0:T(1,128)} %reshape.34), calls=%async_computation.2 | async-start | bytes 262144 | tf_op jit(solution)/shard_map/all_to_all | solution.py:31
  882.5 0.0 copy-done.6
  882.6 0.1 broadcast_in_dim.27
  882.7 13.1 %all-to-all-done = f32[32,1,1024]{2,1,0:T(1,128)S(1)} async-done(((f32[32,1,1024]{2,1,0:T(1,128)}), f32[32,1,1024]{2,1,0:T(1,128)S(1)}, u32[]{:S(2)}, u32[]{:S(2)}) %all-to-all-start) | async-done | bytes 131104 | tf_op jit(solution)/shard_map/all_to_all | solution.py:31
  895.8 0.5 broadcast.27
  896.3 0.9 reduce
  897.3 0.0 copy-start.1
  897.3 0.0 copy-start.2
  897.3 0.0 copy-start.3
  897.3 0.0 copy-start.5
  897.3 0.2 reshape.35
  897.5 0.4 copy.17
  897.9 0.6 gather_fusion
  898.5 0.3 copy.18
  898.8 0.2 gather.7
  899.1 0.0 copy-done.1
  899.1 0.0 copy-done.2
  899.1 0.0 copy-done.3
  899.1 0.0 copy-done.5
  899.1 0.8 fusion.4
  (7 shorter events, 0.1 us)
Async XLA Ops:
  6.5 494.2 %all-reduce.3.cloned.1.call-start = ((), (), s32[]{:S(2)}) async-start(), calls=%async_computation.5 | async-start | bytes 4194304 | tf_op jit(solution)/shard_map/psum | solution.py:13
  9.2 2.8 copy-start.4
  11.9 677.7 %reduce-scatter.3.cloned.1.call-start = ((), (), s32[]{:S(2)}) async-start(), calls=%async_computation.3 | async-start | bytes 2162688 | tf_op jit(solution)/shard_map/reduce_scatter | solution.py:26
  505.3 1.2 copy-start
  505.3 364.4 %reduce-scatter.5.cloned.1.call-start = ((), (), s32[]{:S(2)}) async-start(), calls=%async_computation.4 | async-start | bytes 2162688 | tf_op jit(solution)/shard_map/reduce_scatter | solution.py:26
  510.7 371.8 %copy-start.6 = (s32[32]{0:T(128)S(1)}, s32[32]{0:T(128)}, u32[]{:S(2)}) copy-start(s32[32]{0:T(128)} %param.13) | copy-start | bytes 388
  871.8 24.0 %all-to-all-start = ((f32[32,1,1024]{2,1,0:T(1,128)}), f32[32,1,1024]{2,1,0:T(1,128)S(1)}, u32[]{:S(2)}, u32[]{:S(2)}) async-start(f32[32,1,1024]{2,1,0:T(1,128)} %reshape.34), calls=%async_computation.2 | async-start | bytes 262144 | tf_op jit(solution)/shard_map/all_to_all | solution.py:31
  897.3 1.8 copy-start.1
  897.3 1.8 copy-start.2
  897.3 1.8 copy-start.3
  897.3 1.8 copy-start.5
Sparse Core Ops, SparseCore 0:
  12.0 488.6 all-reduce.2
  506.3 183.2 reduce-scatter.2
  695.2 174.4 reduce-scatter.4
where the time goes:
time: 907 us; the launch traced here: 906 us
  waiting for transfers between devices  858 us (95%)
  between operations  14.6 us (2%)
  starting transfers between devices  10.8 us (1%)
  local copies, waits for them, and re-layouts  9.78 us (1%)
    psum x1, waiting for transfers between devices, spread(): return lax.psum(block, axis)  487 us
    reduce_scatter x2, waiting for transfers between devices, on_device(): lax.psum_scatter(partial_value, 'inpair', scatter_dimension=0, tiled=True)  358 us
  transfers between devices with their start and end apart: 4, of which 4 were waited for; matrix products, arithmetic and copies ran while one was open for 1% of the time, Pallas kernels for 0%

commit v1 on v0

v1 whole, which is shorter than its diff:
```python
import jax
import jax.numpy as jnp
from jax import lax
from jax.experimental import pallas as pl
from jax.experimental.pallas import tpu as pltpu
from jax.sharding import PartitionSpec as P

SUB_R = 256
SUB_C = 256
NB = 2
MESH = pl.DeviceIdType.MESH
LEVELS = 32000.0
F32 = jnp.float32
BF16 = jnp.bfloat16


def quantize(dst, x):
    top = jnp.maximum(jnp.max(jnp.abs(x), axis=1, keepdims=True), 1e-37)
    power = jnp.ceil(jnp.log2(top) * 8.0)
    coded = jnp.round(x * jnp.exp2(power * -0.125) * LEVELS)
    width = x.shape[1]
    dst[:, :width] = coded.astype(jnp.int32).astype(jnp.int16)
    tail = jnp.broadcast_to(power, (x.shape[0], dst.shape[1] - width))
    dst[:, width:] = tail.astype(jnp.int32).astype(jnp.int16)


def restore(src, width):
    power = src[:, width:].astype(jnp.int32).astype(F32)[:, :1]
    scale = jnp.exp2(power * 0.125) * (1.0 / LEVELS)
    return src[:, :width].astype(jnp.int32).astype(F32) * scale


def kernel(owner, mask, v_hbm, a_hbm, out, got, relay, vbuf, mask2, sel, rin, lin, rout, lout, fin, t, part,
           ysend, yrecv, zsend, zrecv,
           a_s, a_r, v_s, v_r, loc, line_s, line_r, ag_s, ag_r, y_s, y_r, z_s, z_r):
    ip = lax.axis_index("inpair")
    op = lax.axis_index("outpair")
    y, zh, c = ip // 8, (ip // 2) % 4, ip % 2
    zl, x = op // 4, op % 4
    xp, xm, xo = (x + 1) % 4, (x + 3) % 4, (x + 2) % 4
    right, left = zl * 4 + xp, zl * 4 + xm
    partner = ip + 1 - 2 * c
    other = 1 - c
    y_up, y_down = (ip + 8) % 32, (ip + 24) % 32
    z_up, z_down = y * 8 + ((zh + 1) % 4) * 2 + c, y * 8 + ((zh + 3) % 4) * 2 + c
    width = v_hbm.shape[1]

    def send(src, dst, s_sem, r_sem, i, o):
        return pltpu.make_async_remote_copy(src_ref=src, dst_ref=dst, send_sem=s_sem, recv_sem=r_sem,
                                            device_id={"inpair": i, "outpair": o}, device_id_type=MESH)

    barrier = pltpu.get_barrier_semaphore()

    def greet(i, o):
        pl.semaphore_signal(barrier, inc=1, device_id={"inpair": i, "outpair": o}, device_id_type=MESH)

    for i in (z_up, z_down, y_up, y_down, partner):
        greet(i, op)
    for o in (right, left):
        greet(ip, o)
        greet(partner, o)

    @pl.when(zl > 0)
    def _():
        greet(ip, op - 4)

    @pl.when(zl < 7)
    def _():
        greet(ip, op + 4)

    load_v = pltpu.make_async_copy(v_hbm, vbuf.at[c], loc.at[0])
    load_v.start()
    load_a = pltpu.make_async_copy(a_hbm.at[0, pl.ds(pl.multiple_of(x * 128, 128), 128)], got.at[x], loc.at[1])
    load_a.start()

    @pl.when(zl == 0)
    def _():
        rin[...] = jnp.zeros_like(rin)

    @pl.when(zl == 7)
    def _():
        lin[...] = jnp.zeros_like(lin)

    pl.semaphore_wait(barrier, 9 + jnp.where(zl > 0, 1, 0) + jnp.where(zl < 7, 1, 0))

    def rows(q, start, n):
        return a_hbm.at[0, pl.ds(pl.multiple_of(q * 128 + start, 64), n)]

    relay_r = send(rows(xo, 0, 64), relay.at[0], a_s.at[0], a_r.at[0], ip, right)
    relay_l = send(rows(xo, 64, 64), relay.at[1], a_s.at[1], a_r.at[1], ip, left)
    full_r = send(rows(xp, 0, 128), got.at[x], a_s.at[2], a_r.at[2], ip, right)
    full_l = send(rows(xm, 0, 128), got.at[x], a_s.at[3], a_r.at[3], ip, left)
    on_r = send(relay.at[0], got.at[xm, pl.ds(0, 64)], a_s.at[4], a_r.at[4], ip, right)
    on_l = send(relay.at[1], got.at[xp, pl.ds(64, 64)], a_s.at[5], a_r.at[5], ip, left)
    for copy in (relay_r, relay_l, full_r, full_l):
        copy.start()
    swap_m = send(mask, mask2, v_s.at[0], v_r.at[0], partner, op)
    swap_v = send(v_hbm, vbuf.at[c], v_s.at[1], v_r.at[1], partner, op)
    swap_m.start()
    swap_v.start()
    relay_r.wait_recv()
    on_r.start()
    relay_l.wait_recv()
    on_l.start()

    def mask_half(half, m):
        for a in range(width // SUB_C):
            at = pl.ds(a * SUB_R, SUB_R)
            vbuf[half, at, :] = vbuf[half, at, :] * m[a:a + 1, :].astype(BF16)

    load_v.wait()
    mask_half(c, mask)
    load_a.wait()
    for copy in (full_r, full_l, on_r, on_l):
        copy.wait_recv()

    def select(k, carry):
        row = (k % 4) * 32 + (c + (k // 4) * (1 - 2 * c)) * 16
        for b in range(NB):
            holder = owner[b]
            here = jnp.where((holder >> 2) == zl, 1.0, 0.0)
            value = got[holder & 3, pl.ds(pl.multiple_of(row, 16), 16), :]
            sel[k, b * 16:(b + 1) * 16, :] = (value.astype(F32) * here).astype(BF16)
        return carry

    lax.fori_loop(0, 8, select, 0)

    far = jnp.maximum(zl, 7 - zl)

    def line_r_copy(k):
        return send(rout.at[k], rin.at[k], line_s.at[0, k], line_r.at[0, k], ip, op + 4)

    def line_l_copy(k):
        return send(lout.at[k], lin.at[k], line_s.at[1, k], line_r.at[1, k], ip, op - 4)

    def ag_copies(k):
        part_k = k // 4
        core = c + part_k * (1 - 2 * c)
        dst = t.at[c, x, pl.ds(pl.multiple_of((k % 4) * 32, 32), 32)]
        to = ip - c + core
        return (send(fin.at[k], dst, ag_s.at[0, k], ag_r.at[0, k], to, right),
                send(fin.at[k], dst, ag_s.at[1, k], ag_r.at[1, k], to, left))

    def pass_on(k, direction):
        half = c + (k // 4) * (1 - 2 * c)
        at = pl.ds(pl.multiple_of((k % 4) * 32, 32), 32)
        if direction == 0:
            return send(t.at[half, xm, at], t.at[half, xm, at], ag_s.at[2, k], ag_r.at[2, k], ip, right)
        return send(t.at[half, xp, at], t.at[half, xp, at], ag_s.at[2, k], ag_r.at[2, k], ip, left)

    def to_partner(k):
        dst = t.at[c, x, pl.ds(pl.multiple_of((k % 4) * 32, 32), 32)]
        return send(fin.at[k], dst, ag_s.at[3, k], ag_r.at[3, k], partner, op)

    lag = 2

    def line(step, carry):
        kr = step - zl

        @pl.when(jnp.logical_and(kr >= 0, kr < 8))
        def _():
            @pl.when(zl > 0)
            def _():
                line_r_copy(kr).wait_recv()

            @pl.when(zl < 7)
            def _():
                rout[kr] = sel[kr] + rin[kr]
                line_r_copy(kr).start()

        kl = step - (7 - zl)

        @pl.when(jnp.logical_and(kl >= 0, kl < 8))
        def _():
            @pl.when(zl < 7)
            def _():
                line_l_copy(kl).wait_recv()

            @pl.when(zl > 0)
            def _():
                lout[kl] = sel[kl] + lin[kl]
                line_l_copy(kl).start()

        kf = step - far

        @pl.when(jnp.logical_and(kf >= 0, kf < 8))
        def _():
            value = sel[kf] + rin[kf] + lin[kf]
            fin[kf] = value

            @pl.when(kf < 4)
            def _():
                t[c, x, pl.ds(pl.multiple_of((kf % 4) * 32, 32), 32), :] = value

            @pl.when(kf >= 4)
            def _():
                to_partner(kf).start()

            for copy in ag_copies(kf):
                copy.start()

        kp = step - far - lag

        @pl.when(jnp.logical_and(kp >= 0, kp < 8))
        def _():
            @pl.when(kp % 2 == 0)
            def _():
                ag_copies(kp)[0].wait_recv()
                pass_on(kp, 0).start()

            @pl.when(kp % 2 == 1)
            def _():
                ag_copies(kp)[1].wait_recv()
                pass_on(kp, 1).start()

        return carry

    lax.fori_loop(0, 15 + lag, line, 0)

    swap_m.wait_recv()
    swap_v.wait_recv()
    mask_half(other, mask2)

    def arrived(k, carry):
        @pl.when(k % 2 == 0)
        def _():
            ag_copies(k)[1].wait_recv()
            pass_on(k, 0).wait_recv()

        @pl.when(k % 2 == 1)
        def _():
            ag_copies(k)[0].wait_recv()
            pass_on(k, 1).wait_recv()

        @pl.when(k >= 4)
        def _():
            to_partner(k).wait_recv()

        return carry

    lax.fori_loop(0, 8, arrived, 0)

    def product(n, carry):
        at = pl.ds(pl.multiple_of(n * 256, 256), 256)
        total = jnp.dot(t[0].reshape(512, 1024), vbuf[0, :, at], preferred_element_type=F32)
        total = total + jnp.dot(t[1].reshape(512, 1024), vbuf[1, :, at], preferred_element_type=F32)
        part[:, :, at] = total.reshape(4, 128, 256)
        return carry

    lax.fori_loop(0, width // 256, product, 0)

    def tree(piece, sendbuf, recvbuf, s_sem, r_sem, up, down):
        def copy(m, to):
            return send(sendbuf.at[m], recvbuf.at[m], s_sem.at[m], r_sem.at[m], to, op)

        copies = [copy(m, (up, down)[m % 2]) for m in (0, 1, 2, 3, 4, 5)]
        first = ((2, 0), (2, 1), (1, 1), (3, 0))
        for m in range(4):
            quantize(sendbuf.at[m], piece(*first[m]))
            copies[m].start()
        for m, which in ((4, (1, 0)), (5, (3, 1))):
            copies[m - 4].wait_recv()
            quantize(sendbuf.at[m], piece(*which) + restore(recvbuf.at[m - 4], width))
            copies[m].start()
        return copies, ((3, 4), (2, 5))

    def y_piece(d, h):
        return part[(y + d) % 4, h * 64:(h + 1) * 64, :]

    y_copies, order = tree(y_piece, ysend, yrecv, y_s, y_r, y_up, y_down)
    for h in range(2):
        value = y_piece(0, h)
        for m in order[h]:
            y_copies[m].wait_recv()
            value = value + restore(yrecv.at[m], width)
        part[y, h * 64:(h + 1) * 64, :] = value

    def z_piece(d, h):
        return part[y, pl.ds(pl.multiple_of(((zh + d) % 4) * 32 + h * 16, 16), 16), :]

    z_copies, order = tree(z_piece, zsend, zrecv, z_s, z_r, z_up, z_down)
    for h in range(2):
        value = z_piece(0, h)
        for m in order[h]:
            z_copies[m].wait_recv()
            value = value + restore(zrecv.at[m], width)
        out[h] = value

    for copy in (relay_r, relay_l, full_r, full_l, on_r, on_l, swap_m, swap_v, *y_copies, *z_copies):
        copy.wait_send()

    def drained(k, carry):
        @pl.when(zl < 7)
        def _():
            line_r_copy(k).wait_send()

        @pl.when(zl > 0)
        def _():
            line_l_copy(k).wait_send()

        for copy in ag_copies(k):
            copy.wait_send()

        @pl.when(k % 2 == 0)
        def _():
            pass_on(k, 0).wait_send()

        @pl.when(k % 2 == 1)
        def _():
            pass_on(k, 1).wait_send()

        @pl.when(k >= 4)
        def _():
            to_partner(k).wait_send()

        return carry

    lax.fori_loop(0, 8, drained, 0)


def contract(owner, mask, integrals, amplitudes):
    any_spec = pl.BlockSpec(memory_space=pl.ANY)
    vmem = pl.BlockSpec(memory_space=pltpu.VMEM)
    dma = pltpu.SemaphoreType.DMA
    return pl.pallas_call(
        kernel,
        out_shape=jax.ShapeDtypeStruct((NB, 16, 1024), F32),
        in_specs=[pl.BlockSpec(memory_space=pltpu.SMEM), vmem, any_spec, any_spec],
        out_specs=vmem,
        scratch_shapes=[
            pltpu.VMEM((4, 128, 1024), BF16),
            pltpu.VMEM((2, 64, 1024), BF16),
            pltpu.VMEM((2, 1024, 1024), BF16),
            pltpu.VMEM((8, 1024), F32),
            *[pltpu.VMEM((8, 32, 1024), BF16)] * 6,
            pltpu.VMEM((2, 4, 128, 1024), BF16),
            pltpu.VMEM((4, 128, 1024), F32),
            *[pltpu.VMEM((6, 64, 1152), jnp.int16)] * 2,
            *[pltpu.VMEM((6, 16, 1152), jnp.int16)] * 2,
            dma((6,)), dma((6,)), dma((2,)), dma((2,)), dma((2,)),
            dma((2, 8)), dma((2, 8)), dma((4, 8)), dma((4, 8)),
            dma((6,)), dma((6,)), dma((6,)), dma((6,)),
        ],
        compiler_params=pltpu.CompilerParams(collective_id=0, has_side_effects=True, vmem_limit_bytes=48 * 1024 * 1024),
    )(owner, mask, integrals, amplitudes)


def on_device(integrals, amplitudes, tile_live, batch_owner, occ_energy, vir_energy, swap_within):
    parties = lax.axis_size("outpair")
    mask = jnp.repeat(jnp.pad(tile_live, ((0, 4), (0, 0))), SUB_C, 1).astype(F32)
    summed = contract(batch_owner, mask, integrals, amplitudes)
    local_rows = summed.shape[1]
    width = summed.shape[2]
    pair_grid = summed.reshape(NB, local_rows, parties, width // parties)
    received = lax.all_to_all(pair_grid, "outpair", split_axis=2, concat_axis=2, tiled=True)
    swapped = jnp.take(received, swap_within, axis=3).reshape(NB, local_rows, width)
    denominator = vir_energy[None, None, :] - occ_energy[:, :, None]
    return (summed + swapped) / denominator


def solution(mesh):
    return jax.shard_map(
        on_device,
        mesh=mesh,
        in_specs=(
            P("inpair", "outpair"),
            P("outpair", None, "inpair"),
            P("inpair", "outpair"),
            P(),
            P(None, "inpair"),
            P("outpair"),
            P(),
        ),
        out_specs=P(None, "inpair", "outpair"),
        check_vma=False,
    )
```

time: 907 us -> 160 us (0.18)
  the two profiles are of different devices: /device:TPU:8 before, /device:TPU:24 now
where the time goes in v1:
time: 160 us
  Pallas kernels  128 us (80%)
  waiting for transfers between devices  14.2 us (9%)
  starting transfers between devices  8.41 us (5%)
  local copies, waits for them, and re-layouts  8.07 us (5%)
  other arithmetic  1.73 us (1%)
    pallas_call x1, Pallas kernels, contract(): pl.pallas_call(kernel, out_shape=jax.ShapeDtypeStruct((NB, 16, 1024), F32...  128 us
    all_to_all x1, waiting for transfers between devices, on_device(): lax.all_to_all(pair_grid, 'outpair', split_axis=2, concat_axis=2, tiled=T...  14.2 us
    all_to_all x1, starting transfers between devices, on_device(): lax.all_to_all(pair_grid, 'outpair', split_axis=2, concat_axis=2, tiled=T...  8.41 us
    unnamed x15, local copies, waits for them, and re-layouts  5.33 us
  transfers between devices with their start and end apart: 1, of which 1 were waited for; matrix products, arithmetic and copies ran while one was open for 0% of the time, Pallas kernels for 0%

profile of v1, /device:TPU:24, one launch (start us, length us, event | category | flops | bytes accessed | tf_op | source)
XLA Modules:
  0.0 160.2 jit_solution(1164946789199727609)
XLA Ops:
  0.0 0.8 copy.20
  0.8 0.1 broadcast_in_dim.21
  0.8 0.0 copy-start
  0.9 1.6 copy-done
  2.4 0.0 copy-start.1
  2.4 1.2 copy-done.1
  3.7 0.0 copy-start.2
  3.7 0.7 copy-done.2
  4.3 127.7 %shard_map.73 = f32[2,16,1024]{2,1,0:T(8,128)S(1)} custom-call(s32[2]{0:T(128)S(1)} %copy-done.2, f32[8,1024]{1,0:T(8,128)S(1)} %bitcast.8, bf16[1024,1024]{1,0:T(8,128)(2,1)S(1)} %copy-done, bf16[1,512,1024]{2,1,0:T(8,128)(2,1)S(1)} %copy-done.1), custom_call_target="tpu_custom_call" | custom-call | tf_op jit(solution)/shard_map/pallas_call | solution.py:325
  132.0 0.0 copy-start.5
  132.0 0.2 reshape.15
  132.2 0.3 copy.25
  132.5 0.9 reshape.25
  133.4 8.4 %all-to-all-start = ((f32[32,1,1024]{2,1,0:T(1,128)}), f32[32,1,1024]{2,1,0:T(1,128)S(1)}, u32[]{:S(2)}, u32[]{:S(2)}) async-start(f32[32,1,1024]{2,1,0:T(1,128)} %reshape.25), calls=%async_computation | async-start | bytes 262144 | tf_op jit(solution)/shard_map/all_to_all | solution.py:355
  141.8 0.0 copy-done.5
  141.9 0.1 broadcast_in_dim.23
  142.0 14.2 %all-to-all-done = f32[32,1,1024]{2,1,0:T(1,128)S(1)} async-done(((f32[32,1,1024]{2,1,0:T(1,128)}), f32[32,1,1024]{2,1,0:T(1,128)S(1)}, u32[]{:S(2)}, u32[]{:S(2)}) %all-to-all-start) | async-done | bytes 131104 | tf_op jit(solution)/shard_map/all_to_all | solution.py:355
  156.1 0.5 broadcast.15
  156.6 0.9 reduce
  157.6 0.0 copy-start.3
  157.6 0.0 copy-start.4
  157.6 0.2 reshape.26
  157.8 0.4 copy.22
  158.3 0.6 gather_fusion
  158.8 0.3 copy.23
  159.2 0.2 gather.7
  159.4 0.0 copy-done.3
  159.4 0.0 copy-done.4
  159.4 0.7 subtract_divide_fusion
  (5 shorter events, 0.0 us)
Async XLA Ops:
  0.8 1.6 copy-start
  2.4 1.2 copy-start.1
  3.7 0.7 copy-start.2
  132.0 9.8 %copy-start.5 = (s32[32]{0:T(128)S(1)}, s32[32]{0:T(128)}, u32[]{:S(2)}) copy-start(s32[32]{0:T(128)} %param.13) | copy-start | bytes 388
  133.4 22.7 %all-to-all-start = ((f32[32,1,1024]{2,1,0:T(1,128)}), f32[32,1,1024]{2,1,0:T(1,128)S(1)}, u32[]{:S(2)}, u32[]{:S(2)}) async-start(f32[32,1,1024]{2,1,0:T(1,128)} %reshape.25), calls=%async_computation | async-start | bytes 262144 | tf_op jit(solution)/shard_map/all_to_all | solution.py:355
  157.6 1.8 %copy-start.3 = (f32[1024]{0:T(1024)S(1)}, f32[1024]{0:T(1024)}, u32[]{:S(2)}) copy-start(f32[1024]{0:T(1024)} %param.12) | copy-start | bytes 12292
  157.6 1.8 %copy-start.4 = (f32[2,16]{1,0:T(2,128)S(1)}, f32[2,16]{1,0:T(2,128)}, u32[]{:S(2)}) copy-start(f32[2,16]{1,0:T(2,128)} %param.11) | copy-start | bytes 388

commit v2 on v1

v2 whole, which is shorter than its diff:
```python
import jax
import jax.numpy as jnp
from jax import lax
from jax.experimental import pallas as pl
from jax.experimental.pallas import tpu as pltpu
from jax.sharding import PartitionSpec as P

SUB_R = 256
SUB_C = 256
NB = 2
GRP = 32
CH = 16
SUBS = 32 // CH
NCH = 8 * SUBS
LAG = 5
HOP = 4
VMEM_LIMIT = 62 * 1024 * 1024
MESH = pl.DeviceIdType.MESH
LEVELS = 32000.0
F32 = jnp.float32
BF16 = jnp.bfloat16


def quantize(dst, x):
    top = jnp.maximum(jnp.max(jnp.abs(x), axis=1, keepdims=True), 1e-37)
    power = jnp.ceil(jnp.log2(top) * 8.0)
    coded = jnp.round(x * jnp.exp2(power * -0.125) * LEVELS)
    width = x.shape[1]
    dst[:, :width] = coded.astype(jnp.int32).astype(jnp.int16)
    tail = jnp.broadcast_to(power, (x.shape[0], dst.shape[1] - width))
    dst[:, width:] = tail.astype(jnp.int32).astype(jnp.int16)


def restore(src, width):
    power = src[:, width:].astype(jnp.int32).astype(F32)[:, :1]
    scale = jnp.exp2(power * 0.125) * (1.0 / LEVELS)
    return src[:, :width].astype(jnp.int32).astype(F32) * scale


def regroup(parts):
    lane = lax.broadcasted_iota(jnp.int32, parts[0].shape, 1) // GRP
    out = []
    for i in range(4):
        value = parts[i]
        for n in range(4):
            if n != i:
                value = jnp.where(lane == n, pltpu.roll(parts[n], ((n - i) * GRP) % 128, axis=1), value)
        out.append(value)
    return out


def kernel(owner, live, swap, v_hbm, a_hbm, out, mask, got, relay, vbuf, mask2, sel, rin, lin, rout, lout, fin, t, part,
           ysend, yrecv, zsend, zrecv, mine, d1, d2s, d2r,
           a_s, a_r, v_s, v_r, loc, line_s, line_r, ag_s, ag_r, y_s, y_r, z_s, z_r, d1_s, d1_r, d2_sem, d2_rem):
    ip = lax.axis_index("inpair")
    op = lax.axis_index("outpair")
    y, zh, c = ip // 8, (ip // 2) % 4, ip % 2
    zl, x = op // 4, op % 4
    xp, xm, xo = (x + 1) % 4, (x + 3) % 4, (x + 2) % 4
    right, left, across = zl * 4 + xp, zl * 4 + xm, zl * 4 + xo
    partner = ip + 1 - 2 * c
    other = 1 - c
    y_up, y_down = (ip + 8) % 32, (ip + 24) % 32
    z_up, z_down = y * 8 + ((zh + 1) % 4) * 2 + c, y * 8 + ((zh + 3) % 4) * 2 + c
    width = v_hbm.shape[1]

    def send(src, dst, s_sem, r_sem, i, o):
        return pltpu.make_async_remote_copy(src_ref=src, dst_ref=dst, send_sem=s_sem, recv_sem=r_sem,
                                            device_id={"inpair": i, "outpair": o}, device_id_type=MESH)

    def along(n):
        return ((zl + n) % 8) * 4 + x

    barrier = pltpu.get_barrier_semaphore()

    def greet(i, o):
        pl.semaphore_signal(barrier, inc=1, device_id={"inpair": i, "outpair": o}, device_id_type=MESH)

    for i in (z_up, z_down):
        greet(i, op)
    for n in range(1, 8):
        greet(ip, along(n))
    for i in (y_up, y_down, partner):
        greet(i, op)
    greet(ip, across)
    for o in (right, left):
        greet(ip, o)
        greet(partner, o)

    for a in range(4):
        for b in range(width // SUB_C):
            mask[a:a + 1, b * SUB_C:(b + 1) * SUB_C] = jnp.full((1, SUB_C), live[a, b].astype(F32), F32)
    mask[4:8, :] = jnp.zeros((4, width), F32)

    load_v = pltpu.make_async_copy(v_hbm, vbuf.at[c], loc.at[0])
    load_v.start()
    load_a = pltpu.make_async_copy(a_hbm.at[0, pl.ds(pl.multiple_of(x * 128, 128), 128)], got.at[x], loc.at[1])
    load_a.start()

    @pl.when(zl == 0)
    def _():
        rin[...] = jnp.zeros_like(rin)

    @pl.when(zl == 7)
    def _():
        lin[...] = jnp.zeros_like(lin)

    pl.semaphore_wait(barrier, 17)

    def quarter(j):
        return (zh + 2 - j + jnp.where(j == 2, 3, 0) + jnp.where(j == 3, 1, 0) + 4) % 4

    def rows(q, j, start, n):
        return a_hbm.at[0, pl.ds(pl.multiple_of(q * 128 + quarter(j) * 32 + start, 16), n)]

    def in_got(q, j, start, n):
        return got.at[q, pl.ds(pl.multiple_of(quarter(j) * 32 + start, 16), n)]

    def relays(j):
        return (send(rows(xo, j, 0, 16), relay.at[0, j], a_s.at[0, j], a_r.at[0, j], ip, right),
                send(rows(xo, j, 16, 16), relay.at[1, j], a_s.at[1, j], a_r.at[1, j], ip, left))

    def fulls(j):
        return (send(rows(xp, j, 0, 32), in_got(x, j, 0, 32), a_s.at[2, j], a_r.at[2, j], ip, right),
                send(rows(xm, j, 0, 32), in_got(x, j, 0, 32), a_s.at[3, j], a_r.at[3, j], ip, left))

    def onward(j):
        return (send(relay.at[0, j], in_got(xm, j, 0, 16), a_s.at[4, j], a_r.at[4, j], ip, right),
                send(relay.at[1, j], in_got(xp, j, 16, 16), a_s.at[5, j], a_r.at[5, j], ip, left))

    def start_relays(j, carry):
        for copy in relays(j):
            copy.start()
        return carry

    def start_fulls(j, carry):
        for copy in fulls(j):
            copy.start()
        return carry

    def start_onward(j, carry):
        for copy, was in zip(onward(j), relays(j)):
            was.wait_recv()
            copy.start()
        return carry

    lax.fori_loop(0, 4, start_relays, 0)
    lax.fori_loop(0, 2, start_fulls, 0)
    swap_m = send(mask, mask2, v_s.at[0], v_r.at[0], partner, op)
    swap_v = send(v_hbm, vbuf.at[c], v_s.at[1], v_r.at[1], partner, op)
    swap_m.start()
    swap_v.start()

    def mask_half(half, m):
        for a in range(width // SUB_C):
            at = pl.ds(a * SUB_R, SUB_R)
            vbuf[half, at, :] = vbuf[half, at, :] * m[a:a + 1, :].astype(BF16)

    load_v.wait()
    mask_half(c, mask)
    lax.fori_loop(0, 2, start_onward, 0)

    def start_rest(j, carry):
        start_fulls(j, 0)
        return start_onward(j, carry)

    lax.fori_loop(2, 4, start_rest, 0)
    load_a.wait()
    swap_m.wait_recv()
    swap_v.wait_recv()
    mask_half(other, mask2)

    def place(k):
        sub, rel = k % SUBS, (k // SUBS) % 2
        return quarter(k // (2 * SUBS)), rel, sub, c + rel * (1 - 2 * c)

    def select(j):
        for copy in (*fulls(j), *onward(j)):
            copy.wait_recv()
        for n in range(2 * SUBS):
            core = c + (n // SUBS) * (1 - 2 * c)
            for part_b in range(CH // 16):
                b = (n % SUBS) if SUBS == 2 else part_b
                holder = owner[b]
                at = pl.ds(pl.multiple_of(quarter(j) * 32 + core * 16, 16), 16)
                value = jnp.zeros((16, width), F32)
                for held in range(4):
                    value = value + got[held, at, :].astype(F32) * jnp.where(holder == zl * 4 + held, 1.0, 0.0)
                sel[j * 2 * SUBS + n, part_b * 16:(part_b + 1) * 16, :] = value.astype(BF16)

    far = HOP * jnp.maximum(zl, 7 - zl)
    near = HOP * jnp.minimum(zl, 7 - zl)

    def line_r_copy(k):
        return send(rout.at[k], rin.at[k], line_s.at[0, k], line_r.at[0, k], ip, op + 4)

    def line_l_copy(k):
        return send(lout.at[k], lin.at[k], line_s.at[1, k], line_r.at[1, k], ip, op - 4)

    def in_t(k, src_x):
        q, _, sub, _ = place(k)
        return q, pl.ds(pl.multiple_of(src_x * 32 + sub * 16, 16), CH)

    def ag_copies(k):
        q, at = in_t(k, x)
        core = place(k)[3]
        dst = t.at[c, q, at]
        to = ip - c + core
        return (send(fin.at[k], dst, ag_s.at[0, k], ag_r.at[0, k], to, right),
                send(fin.at[k], dst, ag_s.at[1, k], ag_r.at[1, k], to, left))

    def pass_on(k, rel):
        if rel == 0:
            q, at = in_t(k, xm)
            return send(t.at[c, q, at], t.at[c, q, at], ag_s.at[2, k], ag_r.at[2, k], ip, right)
        q, at = in_t(k, xp)
        return send(t.at[other, q, at], t.at[other, q, at], ag_s.at[2, k], ag_r.at[2, k], ip, left)

    def to_partner(k):
        q, at = in_t(k, x)
        return send(fin.at[k], t.at[c, q, at], ag_s.at[3, k], ag_r.at[3, k], partner, op)

    def by_kind(k, even, odd):
        rel = (k // SUBS) % 2

        @pl.when(rel == 0)
        def _():
            even()

        @pl.when(rel == 1)
        def _():
            odd()

    def line(step, carry):
        kq = step - near

        @pl.when(jnp.logical_and(jnp.logical_and(kq >= 0, kq < NCH), kq % (2 * SUBS) == 0))
        def _():
            select(kq // (2 * SUBS))

        kr = step - HOP * zl

        @pl.when(jnp.logical_and(kr >= 0, kr < NCH))
        def _():
            @pl.when(zl > 0)
            def _():
                line_r_copy(kr).wait_recv()

            @pl.when(zl < 7)
            def _():
                rout[kr] = sel[kr] + rin[kr]
                line_r_copy(kr).start()

        kl = step - HOP * (7 - zl)

        @pl.when(jnp.logical_and(kl >= 0, kl < NCH))
        def _():
            @pl.when(zl < 7)
            def _():
                line_l_copy(kl).wait_recv()

            @pl.when(zl > 0)
            def _():
                lout[kl] = sel[kl] + lin[kl]
                line_l_copy(kl).start()

        kf = step - far

        @pl.when(jnp.logical_and(kf >= 0, kf < NCH))
        def _():
            value = sel[kf] + rin[kf] + lin[kf]
            fin[kf] = value

            def keep():
                q, at = in_t(kf, x)
                t[c, q, at, :] = value

            by_kind(kf, keep, lambda: to_partner(kf).start())
            for copy in ag_copies(kf):
                copy.start()

        kx = step - far - LAG
        kp = kx - kx // 3

        @pl.when(jnp.logical_and(kx >= 0, kx % 3 != 2))
        def _():
            forward(kp, 0)

        return carry

    def forward(k, carry):
        def even():
            ag_copies(k)[0].wait_recv()
            pass_on(k, 0).start()

        def odd():
            ag_copies(k)[1].wait_recv()
            pass_on(k, 1).start()

        by_kind(k, even, odd)
        return carry

    lax.fori_loop(0, far + NCH, line, 0)
    done = NCH - LAG - (NCH - LAG) // 3

    def arrived(k, carry):
        def even():
            ag_copies(k)[1].wait_recv()
            pass_on(k, 0).wait_recv()

        def odd():
            ag_copies(k)[0].wait_recv()
            pass_on(k, 1).wait_recv()
            to_partner(k).wait_recv()

        by_kind(k, even, odd)
        return carry

    def zq(j):
        return (zh + (2, 1, 3, 0)[j]) % 4

    def product(j):
        lax.fori_loop(2 * SUBS * j, 2 * SUBS * (j + 1), arrived, 0)
        q = zq(j)

        def columns(n, carry):
            at = pl.ds(pl.multiple_of(n * 256, 256), 256)
            total = jnp.dot(t[0, q], vbuf[0, :, at], preferred_element_type=F32)
            total = total + jnp.dot(t[1, q], vbuf[1, :, at], preferred_element_type=F32)
            part[q, :, at] = total
            return carry

        lax.fori_loop(0, width // 256, columns, 0)

    FIRST = ((2, 0), (2, 1), (1, 1), (3, 0))
    SECOND = {4: (1, 0), 5: (3, 1)}
    LAST = ((3, 4), (2, 5))

    def y_copy(j, m):
        return send(ysend.at[j, m], yrecv.at[j, m], y_s.at[j, m], y_r.at[j, m], (y_up, y_down)[m % 2], op)

    def y_piece(j, d, h):
        return part[zq(j), pl.ds(pl.multiple_of(((y + d) % 4) * 32 + h * 16, 16), 16), :]

    def y_first(j):
        for m in range(4):
            quantize(ysend.at[j, m], y_piece(j, *FIRST[m]))
            y_copy(j, m).start()

    def y_second(j):
        for m in (4, 5):
            y_copy(j, m - 4).wait_recv()
            quantize(ysend.at[j, m], y_piece(j, *SECOND[m]) + restore(yrecv.at[j, m - 4], width))
            y_copy(j, m).start()

    def y_last(j):
        values = []
        for h in range(2):
            value = y_piece(j, 0, h)
            for m in LAST[h]:
                y_copy(j, m).wait_recv()
                value = value + restore(yrecv.at[j, m], width)
            values.append(value)
        return values

    def z_copy(m):
        return send(zsend.at[m], zrecv.at[m], z_s.at[m], z_r.at[m], (z_up, z_down)[m % 2], op)

    def z_send(m, value):
        quantize(zsend.at[m], value)
        z_copy(m).start()

    def z_join(value, m):
        z_copy(m).wait_recv()
        return value + restore(zrecv.at[m], width)

    product(0)
    y_first(0)
    lax.fori_loop(done, done + 4, forward, 0)
    product(1)
    y_first(1)
    y_second(0)
    lax.fori_loop(done + 4, NCH, forward, 0)
    product(2)
    y_first(2)
    y_second(1)
    opposite = y_last(0)
    z_send(0, opposite[0])
    z_send(1, opposite[1])
    product(3)
    y_first(3)
    y_second(2)
    above = y_last(1)
    z_send(2, above[1])
    y_second(3)
    below = y_last(2)
    z_send(3, below[0])
    part[zq(1), 0:16, :] = above[0]
    part[zq(2), 0:16, :] = below[1]
    own = y_last(3)
    mine[0:16, :] = own[0]
    mine[16:32, :] = own[1]
    z_send(4, z_join(part[zq(1), 0:16, :], 0))
    z_send(5, z_join(part[zq(2), 0:16, :], 1))
    for h in range(2):
        value = mine[h * 16:(h + 1) * 16, :]
        for m in LAST[h]:
            value = z_join(value, m)
        mine[h * 16:(h + 1) * 16, :] = value

    def d1_copy(n):
        at = pl.ds(pl.multiple_of(((zl + n) % 8) * 128, 128), 128)
        return send(mine.at[:, at], d1.at[zl], d1_s.at[n], d1_r.at[n], ip, along(n))

    for n in (4, 3, 5, 2, 6, 1, 7):
        d1_copy(n).start()
    d1[zl] = mine[:, pl.ds(pl.multiple_of(zl * 128, 128), 128)]
    for n in range(1, 8):
        d1_copy(n).wait_recv()
    packed = regroup([d1[:, r * 8:(r + 1) * 8, :].reshape(64, 128) for r in range(4)])
    for i in range(4):
        d2s[i] = packed[i]

    def d2_copy(n, to):
        return send(d2s.at[(x + n) % 4], d2r.at[x], d2_sem.at[n], d2_rem.at[n], ip, to)

    d2_copies = [d2_copy(2, across), d2_copy(1, right), d2_copy(3, left)]
    for copy in d2_copies:
        copy.start()
    d2r[x] = d2s[x]
    row = lax.broadcasted_iota(jnp.int32, (128, 128), 0)
    column = lax.broadcasted_iota(jnp.int32, (8, 128), 1)
    target = jnp.zeros((8, 128), jnp.int32)
    for g in range(GRP):
        target = jnp.where(column % GRP == g, swap[g] + (column // GRP) * GRP, target)
    pick = jnp.where(row == target[0:1, :], 1.0, 0.0).astype(BF16)
    for copy in d2_copies:
        copy.wait_recv()
    faced = regroup([d2r[i] for i in range(4)])
    for r in range(4):
        rest = faced[r]
        moved = jnp.zeros((64, 128), F32)
        for _ in range(3):
            piece = rest.astype(BF16)
            rest = rest - piece.astype(F32)
            moved = moved + jnp.dot(piece, pick, preferred_element_type=F32)
        for n in range(8):
            out[r // 2, (r % 2) * 8:(r % 2) * 8 + 8, n * 128:(n + 1) * 128] = (
                mine[r * 8:(r + 1) * 8, n * 128:(n + 1) * 128] + moved[n * 8:(n + 1) * 8, :])

    for copy in (swap_m, swap_v, *d2_copies):
        copy.wait_send()
    for n in range(1, 8):
        d1_copy(n).wait_send()
    for m in range(6):
        z_copy(m).wait_send()

    def drained_quarter(j, carry):
        for copy in (*relays(j), *fulls(j), *onward(j)):
            copy.wait_send()
        for m in range(6):
            y_copy(j, m).wait_send()
        return carry

    lax.fori_loop(0, 4, drained_quarter, 0)

    def drained(k, carry):
        @pl.when(zl < 7)
        def _():
            line_r_copy(k).wait_send()

        @pl.when(zl > 0)
        def _():
            line_l_copy(k).wait_send()

        for copy in ag_copies(k):
            copy.wait_send()

        def odd():
            pass_on(k, 1).wait_send()
            to_partner(k).wait_send()

        by_kind(k, lambda: pass_on(k, 0).wait_send(), odd)
        return carry

    lax.fori_loop(0, NCH, drained, 0)


def contract(owner, live, swap, integrals, amplitudes):
    any_spec = pl.BlockSpec(memory_space=pl.ANY)
    vmem = pl.BlockSpec(memory_space=pltpu.VMEM)
    dma = pltpu.SemaphoreType.DMA
    return pl.pallas_call(
        kernel,
        out_shape=jax.ShapeDtypeStruct((NB, 16, 1024), F32),
        in_specs=[pl.BlockSpec(memory_space=pltpu.SMEM)] * 3 + [any_spec, any_spec],
        out_specs=vmem,
        scratch_shapes=[
            pltpu.VMEM((8, 1024), F32),
            pltpu.VMEM((4, 128, 1024), BF16),
            pltpu.VMEM((2, 4, 16, 1024), BF16),
            pltpu.VMEM((2, 1024, 1024), BF16),
            pltpu.VMEM((8, 1024), F32),
            *[pltpu.VMEM((NCH, CH, 1024), BF16)] * 6,
            pltpu.VMEM((2, 4, 128, 1024), BF16),
            pltpu.VMEM((4, 128, 1024), F32),
            *[pltpu.VMEM((4, 6, 16, 1152), jnp.int16)] * 2,
            *[pltpu.VMEM((6, 16, 1152), jnp.int16)] * 2,
            pltpu.VMEM((32, 1024), F32),
            pltpu.VMEM((8, 32, 128), F32),
            *[pltpu.VMEM((4, 64, 128), F32)] * 2,
            dma((6, 4)), dma((6, 4)), dma((2,)), dma((2,)), dma((2,)),
            dma((2, NCH)), dma((2, NCH)), dma((4, NCH)), dma((4, NCH)),
            dma((4, 6)), dma((4, 6)), dma((6,)), dma((6,)),
            dma((8,)), dma((8,)), dma((4,)), dma((4,)),
        ],
        compiler_params=pltpu.CompilerParams(collective_id=0, has_side_effects=True,
                                             vmem_limit_bytes=VMEM_LIMIT),
    )(owner, live, swap, integrals, amplitudes)


def on_device(integrals, amplitudes, tile_live, batch_owner, occ_energy, vir_energy, swap_within):
    both = contract(batch_owner, tile_live, swap_within, integrals, amplitudes)
    return both / (vir_energy[None, None, :] - occ_energy[:, :, None])


def solution(mesh):
    return jax.shard_map(
        on_device,
        mesh=mesh,
        in_specs=(
            P("inpair", "outpair"),
            P("outpair", None, "inpair"),
            P("inpair", "outpair"),
            P(),
            P(None, "inpair"),
            P("outpair"),
            P(),
        ),
        out_specs=P(None, "inpair", "outpair"),
        check_vma=False,
    )
```

time: 160 us -> 120 us (0.75)
  the two profiles are of different devices: /device:TPU:24 before, /device:TPU:2 now
where the time goes in v2:
time: 120 us; the launch traced here: 119 us
  Pallas kernels  118 us (98%)
  other arithmetic  1.65 us (1%)
    pallas_call x1, Pallas kernels, contract(): pl.pallas_call(kernel, out_shape=jax.ShapeDtypeStruct((NB, 16, 1024), F32...  118 us

profile of v2, /device:TPU:2, one launch (start us, length us, event | category | flops | bytes accessed | tf_op | source)
XLA Modules:
  0.0 119.5 jit_solution(945352195805797966)
XLA Ops:
  0.0 0.0 copy-start
  0.0 0.0 copy-start.1
  0.0 117.8 %shard_map.73 = f32[2,16,1024]{2,1,0:T(8,128)} custom-call(s32[2]{0:T(128)} %owner.1, s32[4,4]{1,0:T(4,128)} %live.1, s32[32]{0:T(128)} %swap.1, bf16[1024,1024]{1,0:T(8,128)(2,1)} %v_hbm.1, bf16[1,512,1024]{2,1,0:T(8,128)(2,1)} %a_hbm.1), custom_call_target="tpu_custom_call" | custom-call | tf_op jit(solution)/shard_map/pallas_call | solution.py:493
  117.8 0.0 copy-done
  117.8 0.0 copy-done.1
  117.8 1.7 %subtract_divide_fusion = f32[2,16,1024]{2,1,0:T(8,128)} fusion(f32[2,16,1024]{2,1,0:T(8,128)} %shard_map.73, f32[2,16]{1,0:T(2,128)S(1)} %copy-done.1, f32[1024]{0:T(1024)S(1)} %copy-done), kind=kLoop, calls=%fused_computation | loop fusion | flops 65536 | bytes 266368 | tf_op jit(solution)/shard_map/div | solution.py:524
Async XLA Ops:
  0.0 117.8 %copy-start = (f32[1024]{0:T(1024)S(1)}, f32[1024]{0:T(1024)}, u32[]{:S(2)}) copy-start(f32[1024]{0:T(1024)} %param.12) | copy-start | bytes 12292
  0.0 117.8 %copy-start.1 = (f32[2,16]{1,0:T(2,128)S(1)}, f32[2,16]{1,0:T(2,128)}, u32[]{:S(2)}) copy-start(f32[2,16]{1,0:T(2,128)} %param.11) | copy-start | bytes 388

commit v3 on v2

--- a/solution.py
+++ b/solution.py
@@ -83,6 +83,7 @@
     for i in (y_up, y_down, partner):
         greet(i, op)
     greet(ip, across)
+    greet(partner, across)
     for o in (right, left):
         greet(ip, o)
         greet(partner, o)
@@ -105,7 +106,7 @@
     def _():
         lin[...] = jnp.zeros_like(lin)
 
-    pl.semaphore_wait(barrier, 17)
+    pl.semaphore_wait(barrier, 18)
 
     def quarter(j):
         return (zh + 2 - j + jnp.where(j == 2, 3, 0) + jnp.where(j == 3, 1, 0) + 4) % 4
@@ -144,8 +145,9 @@
             copy.start()
         return carry
 
-    lax.fori_loop(0, 4, start_relays, 0)
-    lax.fori_loop(0, 2, start_fulls, 0)
+    lax.fori_loop(0, 1, start_relays, 0)
+    lax.fori_loop(0, 1, start_fulls, 0)
+    lax.fori_loop(1, 4, start_relays, 0)
     swap_m = send(mask, mask2, v_s.at[0], v_r.at[0], partner, op)
     swap_v = send(v_hbm, vbuf.at[c], v_s.at[1], v_r.at[1], partner, op)
     swap_m.start()
@@ -158,17 +160,14 @@
 
     load_v.wait()
     mask_half(c, mask)
-    lax.fori_loop(0, 2, start_onward, 0)
+    lax.fori_loop(0, 1, start_onward, 0)
 
     def start_rest(j, carry):
         start_fulls(j, 0)
         return start_onward(j, carry)
 
-    lax.fori_loop(2, 4, start_rest, 0)
+    lax.fori_loop(1, 4, start_rest, 0)
     load_a.wait()
-    swap_m.wait_recv()
-    swap_v.wait_recv()
-    mask_half(other, mask2)
 
     def place(k):
         sub, rel = k % SUBS, (k // SUBS) % 2
@@ -209,12 +208,10 @@
         return (send(fin.at[k], dst, ag_s.at[0, k], ag_r.at[0, k], to, right),
                 send(fin.at[k], dst, ag_s.at[1, k], ag_r.at[1, k], to, left))
 
-    def pass_on(k, rel):
-        if rel == 0:
-            q, at = in_t(k, xm)
-            return send(t.at[c, q, at], t.at[c, q, at], ag_s.at[2, k], ag_r.at[2, k], ip, right)
-        q, at = in_t(k, xp)
-        return send(t.at[other, q, at], t.at[other, q, at], ag_s.at[2, k], ag_r.at[2, k], ip, left)
+    def far_copy(k):
+        q, at = in_t(k, x)
+        to = ip - c + place(k)[3]
+        return send(fin.at[k], t.at[c, q, at], ag_s.at[2, k], ag_r.at[2, k], to, across)
 
     def to_partner(k):
         q, at = in_t(k, x)
@@ -231,7 +228,15 @@
         def _():
             odd()
 
+    spare = jnp.where(near >= 2 * HOP, 0, near + NCH + 1)
+
     def line(step, carry):
+        @pl.when(step == spare)
+        def _():
+            swap_m.wait_recv()
+            swap_v.wait_recv()
+            mask_half(other, mask2)
+
         kq = step - near
 
         @pl.when(jnp.logical_and(jnp.logical_and(kq >= 0, kq < NCH), kq % (2 * SUBS) == 0))
@@ -278,42 +283,16 @@
             by_kind(kf, keep, lambda: to_partner(kf).start())
             for copy in ag_copies(kf):
                 copy.start()
-
-        kx = step - far - LAG
-        kp = kx - kx // 3
-
-        @pl.when(jnp.logical_and(kx >= 0, kx % 3 != 2))
-        def _():
-            forward(kp, 0)
-
-        return carry
-
-    def forward(k, carry):
-        def even():
-            ag_copies(k)[0].wait_recv()
-            pass_on(k, 0).start()
-
-        def odd():
-            ag_copies(k)[1].wait_recv()
-            pass_on(k, 1).start()
-
-        by_kind(k, even, odd)
+            far_copy(kf).start()
+
         return carry
 
     lax.fori_loop(0, far + NCH, line, 0)
-    done = NCH - LAG - (NCH - LAG) // 3
 
     def arrived(k, carry):
-        def even():
-            ag_copies(k)[1].wait_recv()
-            pass_on(k, 0).wait_recv()
-
-        def odd():
-            ag_copies(k)[0].wait_recv()
-            pass_on(k, 1).wait_recv()
-            to_partner(k).wait_recv()
-
-        by_kind(k, even, odd)
+        for copy in (*ag_copies(k), far_copy(k)):
+            copy.wait_recv()
+        by_kind(k, lambda: None, lambda: to_partner(k).wait_recv())
         return carry
 
     def zq(j):
@@ -376,11 +355,9 @@
 
     product(0)
     y_first(0)
-    lax.fori_loop(done, done + 4, forward, 0)
     product(1)
     y_first(1)
     y_second(0)
-    lax.fori_loop(done + 4, NCH, forward, 0)
     product(2)
     y_first(2)
     y_second(1)
@@ -473,14 +450,9 @@
         def _():
             line_l_copy(k).wait_send()
 
-        for copy in ag_copies(k):
+        for copy in (*ag_copies(k), far_copy(k)):
             copy.wait_send()
-
-        def odd():
-            pass_on(k, 1).wait_send()
-            to_partner(k).wait_send()
-
-        by_kind(k, lambda: pass_on(k, 0).wait_send(), odd)
+        by_kind(k, lambda: None, lambda: to_partner(k).wait_send())
         return carry
 
     lax.fori_loop(0, NCH, drained, 0)

time: 120 us -> 117 us (0.975)
  the two profiles are of different devices: /device:TPU:2 before, /device:TPU:8 now
where the time goes in v3:
time: 117 us
  Pallas kernels  115 us (98%)
  other arithmetic  1.65 us (1%)
    pallas_call x1, Pallas kernels, contract(): pl.pallas_call(kernel, out_shape=jax.ShapeDtypeStruct((NB, 16, 1024), F32...  115 us

profile of v3, /device:TPU:8, one launch (start us, length us, event | category | flops | bytes accessed | tf_op | source)
XLA Modules:
  0.0 116.6 jit_solution(10921918689455345939)
XLA Ops:
  0.0 0.0 copy-start
  0.0 0.0 copy-start.1
  0.0 114.9 %shard_map.73 = f32[2,16,1024]{2,1,0:T(8,128)} custom-call(s32[2]{0:T(128)} %owner.1, s32[4,4]{1,0:T(4,128)} %live.1, s32[32]{0:T(128)} %swap.1, bf16[1024,1024]{1,0:T(8,128)(2,1)} %v_hbm.1, bf16[1,512,1024]{2,1,0:T(8,128)(2,1)} %a_hbm.1), custom_call_target="tpu_custom_call" | custom-call | tf_op jit(solution)/shard_map/pallas_call | solution.py:465
  114.9 0.0 copy-done
  114.9 0.0 copy-done.1
  114.9 1.7 %subtract_divide_fusion = f32[2,16,1024]{2,1,0:T(8,128)} fusion(f32[2,16,1024]{2,1,0:T(8,128)} %shard_map.73, f32[2,16]{1,0:T(2,128)S(1)} %copy-done.1, f32[1024]{0:T(1024)S(1)} %copy-done), kind=kLoop, calls=%fused_computation | loop fusion | flops 65536 | bytes 266368 | tf_op jit(solution)/shard_map/div | solution.py:496
Async XLA Ops:
  0.0 114.9 %copy-start = (f32[1024]{0:T(1024)S(1)}, f32[1024]{0:T(1024)}, u32[]{:S(2)}) copy-start(f32[1024]{0:T(1024)} %param.12) | copy-start | bytes 12292
  0.0 114.9 %copy-start.1 = (f32[2,16]{1,0:T(2,128)S(1)}, f32[2,16]{1,0:T(2,128)}, u32[]{:S(2)}) copy-start(f32[2,16]{1,0:T(2,128)} %param.11) | copy-start | bytes 388
